TPU v7x, 32 devices: a whole 2x2x4 slice. The times are simulated.
32 devices in a mesh: band: 8 (over z, core), grid: 4 (over y, x).
Axes of the slice: x: 2, y: 2, z: 4, core: 2. Of those that a mesh axis runs over, the one named last changes fastest.
Arguments:
- orbitals: float32 [8, 128, 128, 128], P('band', 'grid')
- sources: int32 [4], replicated, may hold values from 0 to 7, as said below
Outputs:
- compressed: float32 [8, 128, 128, 128], P(None, 'grid', 'band')
Inputs may be any that keep to these rules, and one draw needn't show every extreme that they name: `sources`: 4 distinct orbital indices in some order.
All inputs are finite; a program needn't handle non-finite values.
Results may differ from a plain program's by a relative error of at most 0.0003.
Values sent between devices are 32-bit elements; how exact they have to be, the bound alone decides.
A program may use at most 64 MiB of HBM per device.

v0:
```python
import math

import jax
import jax.numpy as jnp
from jax import lax
from jax.sharding import PartitionSpec as P

highest = lax.Precision.HIGHEST


def spread_2(block, axis, owner):
    block = jnp.where(lax.axis_index(axis) == owner, block, jnp.zeros_like(block))
    return lax.psum(block, axis)


def cas_table(length):
    index_values = jnp.arange(length, dtype=jnp.int32)
    products = index_values[:, None] * index_values[None, :] % length
    angles = products.astype(jnp.float32) * (2.0 * math.pi / length)
    return jnp.cos(angles) + jnp.sin(angles)


def squared_waves(start, count, length):
    index_values = start + jnp.arange(count, dtype=jnp.int32)
    signed = jnp.where(index_values < length // 2, index_values, index_values - length)
    waves = signed.astype(jnp.float32) * (2.0 * math.pi / length)
    return waves * waves


def per_device(orbitals, sources):
    band_count, slab_x, full_y, full_z = orbitals.shape
    grid_count = lax.axis_size("grid")
    full_x = slab_x * grid_count
    total_bands = band_count * lax.axis_size("band")
    round_count = sources.shape[0]
    table_x = cas_table(full_x)
    table_y = cas_table(full_y)
    table_z = cas_table(full_z)
    column_y = full_y // grid_count
    start_y = lax.axis_index("grid") * column_y
    waves = (
        squared_waves(0, full_x, full_x)[:, None, None]
        + squared_waves(start_y, column_y, full_y)[None, :, None]
        + squared_waves(0, full_z, full_z)[None, None, :]
    )
    screen = (4.0 * math.pi / full_x) ** 2
    volume = 1.0 / (full_x * full_y * full_z)
    kernel = volume / (waves + screen)

    def plane_transform(field):
        spread = jnp.einsum("bxyz,zk->bxyk", field, table_z, precision=highest)
        return jnp.einsum("bxyk,yj->bxjk", spread, table_y, precision=highest)

    def own_slab(number):
        owner = number // band_count
        local = number % band_count
        return (owner, lax.dynamic_index_in_dim(orbitals, local, 0, keepdims=False))

    def fetch(number):
        owner, slab = own_slab(number)
        return spread_2(slab, "band", owner)

    arrived = [fetch(sources[turn]) for turn in range(round_count)]
    terms = jnp.zeros(orbitals.shape, jnp.float32)
    for turn in range(round_count):
        source = arrived[turn][None]
        spectra = plane_transform(orbitals * source)
        potential_columns = lax.all_to_all(spectra, "grid", split_axis=2, concat_axis=1, tiled=True)
        line_spread = jnp.einsum("bxyz,xa->bayz", potential_columns, table_x, precision=highest)
        line_spread = line_spread * kernel[None]
        filtered = jnp.einsum("bayz,ax->bxyz", line_spread, table_x, precision=highest)
        terms = terms + source * plane_transform(
            lax.all_to_all(filtered, "grid", split_axis=1, concat_axis=2, tiled=True)
        )
    orbital_cols, term_cols = (
        lax.all_to_all(orbitals, "band", split_axis=2, concat_axis=0, tiled=True),
        lax.all_to_all(terms, "band", split_axis=2, concat_axis=0, tiled=True),
    )
    flat_orbitals = orbital_cols.reshape(total_bands, -1)
    flat_terms = term_cols.reshape(total_bands, -1)
    partial_intersection = (
        jnp.dot(flat_orbitals, flat_terms.T, precision=highest, preferred_element_type=jnp.float32)
        * volume
    )
    intersection = lax.psum(partial_intersection, ("band", "grid"))
    factor = jnp.linalg.cholesky(intersection)
    solved = lax.linalg.triangular_solve(factor, flat_terms, left_side=True, lower=True)
    return (-solved).reshape(term_cols.shape)


def solution(mesh):
    placed = (P("band", "grid", None, None), P())
    return jax.shard_map(
        per_device,
        mesh=mesh,
        in_specs=placed,
        out_specs=P(None, "grid", "band", None),
        check_vma=False,
    )
```

profile of v0, /device:TPU:0, one launch (start us, length us, event | category | flops | bytes accessed | tf_op | source)
XLA Modules:
  0.0 616.2 jit_solution(3678246858079370884)
XLA Ops:
  10.5 5.3 broadcast_select_fusion.3
  15.9 178.5 %all-reduce.3.cloned.1.call-done = (f32[1,32,128,128]{3,2,1,0:T(8,128)}, f32[1,32,128,128]{3,2,1,0:T(8,128)}, f32[1,32,128,128]{3,2,1,0:T(8,128)}, f32[1,32,128,128]{3,2,1,0:T(8,128)}) async-done(((f32[1,32,128,128]{3,2,1,0:T(8,128)}, f32[1,32,128,128]{3,2,1,0:T(8,128)}, f32[1,32,128,128]{3,2,1,0:T(8,128)}, f32[1,32,128,128]{3,2,1,0:T(8,128)}), (f32[1,32,128,128]{3,2,1,0:T(8,128)}, ...) | async-done | bytes 8388624 | tf_op jit(solution)/shard_map/psum | solution.py:13
  194.4 3.7 fusion.11
  202.8 4.7 all-to-all-start.2
  207.5 3.7 fusion.13
  213.4 2.6 copy.48
  216.0 16.4 %all-to-all-done.2 = f32[1,32,128,128]{3,1,0,2:T(8,128)} async-done(((f32[1,32,128,128]{3,1,0,2:T(8,128)}), f32[1,32,128,128]{3,1,0,2:T(8,128)}, u32[]{:S(2)}, u32[]{:S(2)}) %all-to-all-start.2) | async-done | bytes 2097184 | tf_op jit(solution)/shard_map/all_to_all | solution.py:68
  232.4 4.5 all-to-all-start
  236.8 3.7 fusion.9
  245.2 16.1 %all-to-all-done = f32[1,32,128,128]{3,1,0,2:T(8,128)} async-done(((f32[1,32,128,128]{3,1,0,2:T(8,128)}), f32[1,32,128,128]{3,1,0,2:T(8,128)}, u32[]{:S(2)}, u32[]{:S(2)}) %all-to-all-start) | async-done | bytes 2097184 | tf_op jit(solution)/shard_map/all_to_all | solution.py:68
  261.3 4.9 all-to-all-start.4
  266.2 3.7 fusion.7
  272.1 2.5 copy.72
  274.7 16.0 %all-to-all-done.4 = f32[1,32,128,128]{3,1,0,2:T(8,128)} async-done(((f32[1,32,128,128]{3,1,0,2:T(8,128)}), f32[1,32,128,128]{3,1,0,2:T(8,128)}, u32[]{:S(2)}, u32[]{:S(2)}) %all-to-all-start.4) | async-done | bytes 2097184 | tf_op jit(solution)/shard_map/all_to_all | solution.py:68
  290.7 4.5 all-to-all-start.6
  295.3 2.8 copy.57
  298.3 3.2 fusion.19
  306.5 13.2 %all-to-all-done.6 = f32[1,32,128,128]{3,1,0,2:T(8,128)} async-done(((f32[1,32,128,128]{3,1,0,2:T(8,128)}), f32[1,32,128,128]{3,1,0,2:T(8,128)}, u32[]{:S(2)}, u32[]{:S(2)}) %all-to-all-start.6) | async-done | bytes 2097184 | tf_op jit(solution)/shard_map/all_to_all | solution.py:68
  319.7 4.6 all-to-all-start.3
  324.3 2.8 copy.49
  327.3 3.2 fusion.21
  333.0 2.5 copy.52
  335.5 13.2 %all-to-all-done.3 = f32[1,128,32,128]{3,2,0,1:T(8,128)} async-done(((f32[1,128,32,128]{3,2,0,1:T(8,128)}), f32[1,128,32,128]{3,2,0,1:T(8,128)}, u32[]{:S(2)}, u32[]{:S(2)}) %all-to-all-start.3) | async-done | bytes 2097184 | tf_op jit(solution)/shard_map/all_to_all | solution.py:73
  348.7 4.7 all-to-all-start.1
  353.4 2.8 copy.65
  356.4 3.2 fusion.17
  364.6 13.2 %all-to-all-done.1 = f32[1,128,32,128]{3,2,0,1:T(8,128)} async-done(((f32[1,128,32,128]{3,2,0,1:T(8,128)}), f32[1,128,32,128]{3,2,0,1:T(8,128)}, u32[]{:S(2)}, u32[]{:S(2)}) %all-to-all-start.1) | async-done | bytes 2097184 | tf_op jit(solution)/shard_map/all_to_all | solution.py:73
  377.9 4.9 all-to-all-start.5
  382.8 2.8 copy.73
  385.8 3.2 fusion.15
  391.5 2.6 copy.76
  395.9 3.2 copy.53
  399.1 3.4 fusion.71
  402.5 4.8 all-to-all-done.5
  407.3 4.6 all-to-all-start.7
  414.1 3.5 fusion.86
  419.8 3.5 fusion.91
  425.4 3.5 fusion.81
  428.9 7.3 %all-to-all-done.7 = f32[1,128,32,128]{3,2,0,1:T(8,128)} async-done(((f32[1,128,32,128]{3,2,0,1:T(8,128)}), f32[1,128,32,128]{3,2,0,1:T(8,128)}, u32[]{:S(2)}, u32[]{:S(2)}) %all-to-all-start.7) | async-done | bytes 2097184 | tf_op jit(solution)/shard_map/all_to_all | solution.py:73
  440.6 6.3 %fusion.3 = f32[1,32,128,128]{3,2,1,0:T(8,128)S(1)} fusion(f32[1,32,128,128]{3,2,1,0:T(8,128)S(1)} %copy-done.1, f32[1,32,128,128]{3,2,1,0:T(8,128)S(1)} %copy-done.2, f32[128,32,128]{2,0,1:T(8,128)} %fusion.81, f32[1,32,128,128]{3,2,1,0:T(8,128)S(1)} %copy-done.3, f32[128,32,128]{2,0,1:T(8,128)} %fusion.86, f32[1,32,128,128]{3,2,1,0:T(8,128)S(1)} %copy-done.4, ...), kind=kOutput, calls=%fused_computation.5 | convolution fusion | flops 809222144 | bytes 18874368 | tf_op jit(solution)/shard_map/bxyk,yj->bxjk/dot_general | solution.py:52
  449.4 4.3 all-to-all-start.8
  453.8 2.6 copy.82
  456.4 46.5 %all-to-all-done.8 = f32[1,32,128,128]{3,1,0,2:T(8,128)} async-done(((f32[1,32,128,128]{3,1,0,2:T(8,128)}), f32[1,32,128,128]{3,1,0,2:T(8,128)}, u32[]{:S(2)}, u32[]{:S(2)}) %all-to-all-start.8) | async-done | bytes 2097184 | tf_op jit(solution)/shard_map/all_to_all | solution.py:77
  502.8 4.6 all-to-all-start.9
  507.4 2.8 copy.81
  510.3 46.2 %all-to-all-done.9 = f32[1,32,128,128]{3,1,0,2:T(8,128)} async-done(((f32[1,32,128,128]{3,1,0,2:T(8,128)}), f32[1,32,128,128]{3,1,0,2:T(8,128)}, u32[]{:S(2)}, u32[]{:S(2)}) %all-to-all-start.9) | async-done | bytes 2097184 | tf_op jit(solution)/shard_map/all_to_all | solution.py:76
  556.5 9.3 %fusion.57 = f32[8,8]{0,1:T(8,128)S(1)} fusion(f32[1,32,8,16,128]{4,1,3,2,0:T(8,128)} %bitcast.64, f32[1,32,8,16,128]{4,1,3,2,0:T(8,128)} %bitcast.61), kind=kOutput, calls=%fused_computation.51 | convolution fusion | flops 50331712 | bytes 4194560 | tf_op jit(solution)/shard_map/dot_general | solution.py:82
  565.8 36.8 %psum.39 = f32[8,8]{0,1:T(8,128)S(1)} all-reduce(f32[8,8]{0,1:T(8,128)S(1)} %fusion.57), channel_id=1, replica_groups=mesh['band'=8,'grid'=4] {'band','grid'}, use_global_device_ids=true, to_apply=%region_4.5 | all-reduce | flops 64 | bytes 512 | tf_op jit(solution)/shard_map/psum | solution.py:85
  (52 shorter events, 52.7 us)
Async XLA Ops:
  6.5 187.8 %all-reduce.3.cloned.1.call-start = ((), (), s32[]{:S(2)}) async-start(), calls=%async_computation.10 | async-start | bytes 16777216 | tf_op jit(solution)/shard_map/psum | solution.py:13
  15.9 178.5 %copy-start = (f32[1,32,128,128]{3,2,1,0:T(8,128)S(1)}, f32[1,32,128,128]{3,2,1,0:T(8,128)}, u32[]{:S(2)}) copy-start(f32[1,32,128,128]{3,2,1,0:T(8,128)} %param.2) | copy-start | bytes 6291460
  202.8 29.6 %all-to-all-start.2 = ((f32[1,32,128,128]{3,1,0,2:T(8,128)}), f32[1,32,128,128]{3,1,0,2:T(8,128)}, u32[]{:S(2)}, u32[]{:S(2)}) async-start(f32[1,32,128,128]{3,1,0,2:T(8,128)} %copy.56), calls=%async_computation.2 | async-start | bytes 4194304 | tf_op jit(solution)/shard_map/all_to_all | solution.py:68
  232.4 29.0 %all-to-all-start = ((f32[1,32,128,128]{3,1,0,2:T(8,128)}), f32[1,32,128,128]{3,1,0,2:T(8,128)}, u32[]{:S(2)}, u32[]{:S(2)}) async-start(f32[1,32,128,128]{3,1,0,2:T(8,128)} %copy.48), calls=%async_computation | async-start | bytes 4194304 | tf_op jit(solution)/shard_map/all_to_all | solution.py:68
  261.3 29.3 %all-to-all-start.4 = ((f32[1,32,128,128]{3,1,0,2:T(8,128)}), f32[1,32,128,128]{3,1,0,2:T(8,128)}, u32[]{:S(2)}, u32[]{:S(2)}) async-start(f32[1,32,128,128]{3,1,0,2:T(8,128)} %copy.64), calls=%async_computation.4 | async-start | bytes 4194304 | tf_op jit(solution)/shard_map/all_to_all | solution.py:68
  290.7 29.0 %all-to-all-start.6 = ((f32[1,32,128,128]{3,1,0,2:T(8,128)}), f32[1,32,128,128]{3,1,0,2:T(8,128)}, u32[]{:S(2)}, u32[]{:S(2)}) async-start(f32[1,32,128,128]{3,1,0,2:T(8,128)} %copy.72), calls=%async_computation.6 | async-start | bytes 4194304 | tf_op jit(solution)/shard_map/all_to_all | solution.py:68
  319.7 29.1 %all-to-all-start.3 = ((f32[1,128,32,128]{3,2,0,1:T(8,128)}), f32[1,128,32,128]{3,2,0,1:T(8,128)}, u32[]{:S(2)}, u32[]{:S(2)}) async-start(f32[1,128,32,128]{3,2,0,1:T(8,128)} %copy.60), calls=%async_computation.3 | async-start | bytes 4194304 | tf_op jit(solution)/shard_map/all_to_all | solution.py:73
  348.7 29.1 %all-to-all-start.1 = ((f32[1,128,32,128]{3,2,0,1:T(8,128)}), f32[1,128,32,128]{3,2,0,1:T(8,128)}, u32[]{:S(2)}, u32[]{:S(2)}) async-start(f32[1,128,32,128]{3,2,0,1:T(8,128)} %copy.52), calls=%async_computation.1 | async-start | bytes 4194304 | tf_op jit(solution)/shard_map/all_to_all | solution.py:73
  377.9 29.4 %all-to-all-start.5 = ((f32[1,128,32,128]{3,2,0,1:T(8,128)}), f32[1,128,32,128]{3,2,0,1:T(8,128)}, u32[]{:S(2)}, u32[]{:S(2)}) async-start(f32[1,128,32,128]{3,2,0,1:T(8,128)} %copy.68), calls=%async_computation.5 | async-start | bytes 4194304 | tf_op jit(solution)/shard_map/all_to_all | solution.py:73
  407.3 29.0 %all-to-all-start.7 = ((f32[1,128,32,128]{3,2,0,1:T(8,128)}), f32[1,128,32,128]{3,2,0,1:T(8,128)}, u32[]{:S(2)}, u32[]{:S(2)}) async-start(f32[1,128,32,128]{3,2,0,1:T(8,128)} %copy.76), calls=%async_computation.7 | async-start | bytes 4194304 | tf_op jit(solution)/shard_map/all_to_all | solution.py:73
  411.9 2.2 copy-start.6
  414.1 3.5 copy-start.5
  436.2 4.4 copy-start.3
  436.2 4.4 copy-start.4
  438.2 2.4 copy-start.1
  438.2 2.4 copy-start.2
  449.4 53.4 %all-to-all-start.8 = ((f32[1,32,128,128]{3,1,0,2:T(8,128)}), f32[1,32,128,128]{3,1,0,2:T(8,128)}, u32[]{:S(2)}, u32[]{:S(2)}) async-start(f32[1,32,128,128]{3,1,0,2:T(8,128)} %copy.79), calls=%async_computation.8 | async-start | bytes 4194304 | tf_op jit(solution)/shard_map/all_to_all | solution.py:77
  502.8 53.6 %all-to-all-start.9 = ((f32[1,32,128,128]{3,1,0,2:T(8,128)}), f32[1,32,128,128]{3,1,0,2:T(8,128)}, u32[]{:S(2)}, u32[]{:S(2)}) async-start(f32[1,32,128,128]{3,1,0,2:T(8,128)} %copy.82), calls=%async_computation.9 | async-start | bytes 4194304 | tf_op jit(solution)/shard_map/all_to_all | solution.py:76
Sparse Core Ops, SparseCore 0:
  16.0 178.3 all-reduce.2
where the time goes:
time: 623 us; the launch traced here: 616 us
  waiting for transfers between devices  371 us (60%)
  matrix products  84.1 us (13%)
  local copies, waits for them, and re-layouts  52.8 us (8%)
  starting transfers between devices  46.3 us (7%)
  blocking collectives  36.8 us (6%)
  between operations  16.8 us (3%)
  other arithmetic  8.11 us (1%)
    psum x1, waiting for transfers between devices, spread_2(): return lax.psum(block, axis)  178 us
    all_to_all x4, waiting for transfers between devices, per_device(): lax.all_to_all(spectra, 'grid', split_axis=2, concat_axis=1, tiled=True)  61.6 us
    all_to_all x1, waiting for transfers between devices, per_device(): lax.all_to_all(terms, 'band', split_axis=2, concat_axis=0, tiled=True)  46.5 us
    all_to_all x1, waiting for transfers between devices, per_device(): lax.all_to_all(orbitals, 'band', split_axis=2, concat_axis=0, tiled=True)  46.2 us
    all_to_all x4, waiting for transfers between devices, per_device(): lax.all_to_all(filtered, 'grid', split_axis=1, concat_axis=2, tiled=True)  38.6 us
    psum x1, blocking collectives, per_device(): intersection = lax.psum(partial_intersection, ('band', 'grid'))  36.8 us
    dot_general x8, matrix products, plane_transform(): return jnp.einsum('bxyk,yj->bxjk', spread, table_y, precision=highest)  25.4 us
    dot_general x8, matrix products, plane_transform(): spread = jnp.einsum('bxyz,zk->bxyk', field, table_z, precision=highest)  24.9 us
  transfers between devices with their start and end apart: 11, of which 11 were waited for; matrix products, arithmetic and copies ran while one was open for 16% of the time, Pallas kernels for 0%

commit v1 on v0

--- a/solution.py
+++ b/solution.py
@@ -1,11 +1,16 @@
+import functools
 import math
 
 import jax
 import jax.numpy as jnp
+import numpy as np
 from jax import lax
+from jax.experimental import pallas as pl
+from jax.experimental.pallas import tpu as pltpu
 from jax.sharding import PartitionSpec as P
 
 highest = lax.Precision.HIGHEST
+MESH = pl.DeviceIdType.MESH
 
 
 def spread_2(block, axis, owner):
@@ -27,7 +32,7 @@
     return waves * waves
 
 
-def per_device(orbitals, sources):
+def general(orbitals, sources):
     band_count, slab_x, full_y, full_z = orbitals.shape
     grid_count = lax.axis_size("grid")
     full_x = slab_x * grid_count
@@ -88,6 +93,423 @@
     return (-solved).reshape(term_cols.shape)
 
 
+def parts_of(value):
+    high = value.astype(jnp.bfloat16)
+    low = (value - high.astype(jnp.float32)).astype(jnp.bfloat16)
+    return high, low
+
+
+def along_rows(left, first, second):
+    n = first.shape[0]
+    h0, l0 = parts_of(first)
+    h1, l1 = parts_of(second)
+    right = jnp.concatenate(
+        [jnp.concatenate([h0, h1], axis=1), jnp.concatenate([l0, l1], axis=1)], axis=0
+    )
+    both = jnp.dot(left, right, preferred_element_type=jnp.float32)
+    return both[:n] + both[n:]
+
+
+def along_lanes(rows, right):
+    n = rows.shape[1]
+    high, low = parts_of(rows)
+    both = jnp.dot(
+        jnp.concatenate([high, low], axis=1), right, preferred_element_type=jnp.float32
+    )
+    return both[:, :n] + both[:, n:]
+
+
+def whole_kernel(
+    bands, grids, rounds, chunks, n, volume, screen,
+    sources, orbitals, left_ref, right_ref, waves_ref, out, *scratch,
+):
+    gath = scratch[:chunks]
+    (spec, cols, back, terms, tcol, part, sums_b, sums_g, splat, in_sem,
+     g_recv, up_send, dn_send, pt_send, f_send, f_recv, b_send, b_recv,
+     t_send, t_recv, sb_send, sb_recv, sg_send, sg_recv) = scratch[chunks:]
+    b = lax.axis_index("band")
+    g = lax.axis_index("grid")
+    nz = bands // 2
+    z, core = b // 2, b % 2
+    slab = n // grids
+    depth = slab // chunks
+    ycols = n // grids
+    piece = ycols * depth
+    yb = n // bands
+    partner = z * 2 + (1 - core)
+
+    barrier = pltpu.get_barrier_semaphore()
+    for d in range(1, bands):
+        pl.semaphore_signal(barrier, inc=1, device_id=(lax.rem(b + d, bands), g), device_id_type=MESH)
+    for d in range(1, grids):
+        pl.semaphore_signal(barrier, inc=1, device_id=(b, lax.rem(g + d, grids)), device_id_type=MESH)
+    loads = [
+        pltpu.make_async_copy(
+            orbitals.at[0, pl.ds(c * depth, depth)], gath[c].at[b], in_sem.at[c]
+        )
+        for c in range(chunks)
+    ]
+    for load in loads:
+        load.start()
+    pl.semaphore_wait(barrier, bands + grids - 2)
+
+    def slab_copy(c, origin, target, send):
+        return pltpu.make_async_remote_copy(
+            src_ref=gath[c].at[origin], dst_ref=gath[c].at[origin],
+            send_sem=send, recv_sem=g_recv.at[origin * chunks + c],
+            device_id=(target, g), device_id_type=MESH,
+        )
+
+    def go_up(c, d):
+        return slab_copy(c, (z - d) * 2 + core, (z + 1) * 2 + core, up_send.at[d * chunks + c])
+
+    def go_down(c, d):
+        return slab_copy(c, (z + d) * 2 + core, (z - 1) * 2 + core, dn_send.at[d * chunks + c])
+
+    def go_partner(c, zz):
+        return slab_copy(c, zz * 2 + core, partner, pt_send.at[zz * chunks + c])
+
+    def own_sends(c):
+        loads[c].wait()
+
+        @pl.when(z + 1 < nz)
+        def _():
+            go_up(c, 0).start()
+
+        @pl.when(z > 0)
+        def _():
+            go_down(c, 0).start()
+
+        go_partner(c, z).start()
+
+    def arrivals(c):
+        for d in range(1, nz):
+            @pl.when(z - d >= 0)
+            def _():
+                slab_copy(c, (z - d) * 2 + core, partner, pt_send.at[0]).wait_recv()
+
+                @pl.when(z + 1 < nz)
+                def _():
+                    go_up(c, d).start()
+
+                go_partner(c, z - d).start()
+
+            @pl.when(z + d < nz)
+            def _():
+                slab_copy(c, (z + d) * 2 + core, partner, pt_send.at[0]).wait_recv()
+
+                @pl.when(z > 0)
+                def _():
+                    go_down(c, d).start()
+
+                go_partner(c, z + d).start()
+
+    def partner_arrivals(c):
+        for zz in range(nz):
+            slab_copy(c, zz * 2 + (1 - core), partner, pt_send.at[0]).wait_recv()
+
+    left = left_ref[...]
+    right = right_ref[...]
+
+    def f_copy(c, r, target, owner):
+        return pltpu.make_async_remote_copy(
+            src_ref=spec.at[c * rounds + r, pl.ds(target * piece, piece)],
+            dst_ref=cols.at[r, owner * chunks + c],
+            send_sem=f_send.at[(c * rounds + r) * grids + target],
+            recv_sem=f_recv.at[(c * rounds + r) * grids + owner],
+            device_id=(b, target), device_id_type=MESH,
+        )
+
+    def b_copy(c, r, target, owner):
+        return pltpu.make_async_remote_copy(
+            src_ref=cols.at[r, target * chunks + c],
+            dst_ref=back.at[c * rounds + r, pl.ds(owner * piece, piece)],
+            send_sem=b_send.at[(c * rounds + r) * grids + target],
+            recv_sem=b_recv.at[(c * rounds + r) * grids + owner],
+            device_id=(b, target), device_id_type=MESH,
+        )
+
+    own_sends(0)
+    for c in range(chunks):
+        arrivals(c)
+        if c + 1 < chunks:
+            own_sends(c + 1)
+        partner_arrivals(c)
+
+        def forward(r, _, c=c):
+            s = sources[r]
+            for k in range(0, depth, 2):
+                pair = gath[c][s, pl.ds(k, 2)] * gath[c][b, pl.ds(k, 2)]
+                rows = along_lanes(pair.reshape(2 * n, n), right)
+                planes = along_rows(left, rows[:n], rows[n:])
+                spec[c * rounds + r, pl.ds(k, n, stride=depth), :] = planes[:, :n]
+                spec[c * rounds + r, pl.ds(k + 1, n, stride=depth), :] = planes[:, n:]
+            for d in range(1, grids):
+                f_copy(c, r, lax.rem(g + d, grids), g).start()
+            cols[r, g * chunks + c] = spec[c * rounds + r, pl.ds(g * piece, piece), :]
+            return 0
+
+        lax.fori_loop(0, rounds, forward, 0)
+
+    base = waves_ref[...]
+    for r in range(rounds):
+        for c in range(chunks):
+            for d in range(1, grids):
+                f_copy(c, r, g, lax.rem(g + d, grids)).wait_recv()
+
+        def line(k, _, r=r):
+            lines = [
+                cols[r, :, pl.ds(pl.multiple_of((2 * k + e) * depth, depth), depth), :].reshape(n, n)
+                for e in range(2)
+            ]
+            moved = along_rows(left, lines[0], lines[1])
+            filtered = []
+            for e in range(2):
+                ky = g * ycols + 2 * k + e
+                signed = jnp.where(ky < n // 2, ky, ky - n).astype(jnp.float32)
+                wave = signed * (2.0 * math.pi / n)
+                filtered.append(moved[:, e * n:(e + 1) * n] * (volume / (base + wave * wave)))
+            done = along_rows(left, filtered[0], filtered[1])
+            for e in range(2):
+                cols[r, :, pl.ds(pl.multiple_of((2 * k + e) * depth, depth), depth), :] = (
+                    done[:, e * n:(e + 1) * n].reshape(grids * chunks, depth, n)
+                )
+            return 0
+
+        lax.fori_loop(0, ycols // 2, line, 0)
+        for d in range(1, grids):
+            b_copy(0, r, lax.rem(g + d, grids), g).start()
+    for c in range(1, chunks):
+        for r in range(rounds):
+            for d in range(1, grids):
+                b_copy(c, r, lax.rem(g + d, grids), g).start()
+
+    def t_copy(c, target, owner):
+        return pltpu.make_async_remote_copy(
+            src_ref=terms.at[pl.ds(c * depth, depth), pl.ds(target * yb, yb)],
+            dst_ref=tcol.at[owner, pl.ds(c * depth, depth)],
+            send_sem=t_send.at[c * bands + target],
+            recv_sem=t_recv.at[c * bands + owner],
+            device_id=(target, g), device_id_type=MESH,
+        )
+
+    def overlap(c):
+        for d in range(1, bands):
+            t_copy(c, b, lax.rem(b + d, bands)).wait_recv()
+
+        def one(i, _):
+            mine = gath[c][i, :, pl.ds(b * yb, yb), :]
+            for k in range(bands):
+                prod = mine * tcol[k, pl.ds(c * depth, depth)]
+                total = jnp.sum(prod.reshape(-1, 8, n), axis=0)
+                if c == 0:
+                    part[i * bands + k] = total
+                else:
+                    part[i * bands + k] += total
+            return 0
+
+        lax.fori_loop(0, bands, one, 0)
+
+    for c in range(chunks):
+        for r in range(rounds):
+            for d in range(1, grids):
+                b_copy(c, r, g, lax.rem(g + d, grids)).wait_recv()
+            back[c * rounds + r, pl.ds(g * piece, piece), :] = cols[r, g * chunks + c]
+            s = sources[r]
+
+            def inverse(k, _, c=c, r=r, s=s):
+                planes = along_rows(
+                    left,
+                    back[c * rounds + r, pl.ds(2 * k, n, stride=depth), :],
+                    back[c * rounds + r, pl.ds(2 * k + 1, n, stride=depth), :],
+                )
+                rows = jnp.concatenate([planes[:, :n], planes[:, n:]], axis=0)
+                potential = along_lanes(rows, right).reshape(2, n, n)
+                here = gath[c][s, pl.ds(2 * k, 2)] * potential
+                if r == 0:
+                    terms[pl.ds(c * depth + 2 * k, 2)] = here
+                else:
+                    terms[pl.ds(c * depth + 2 * k, 2)] += here
+                return 0
+
+            for k in range(depth // 2):
+                inverse(k, 0)
+        for d in range(1, bands):
+            t_copy(c, lax.rem(b + d, bands), b).start()
+        tcol[b, pl.ds(c * depth, depth)] = terms[pl.ds(c * depth, depth), pl.ds(b * yb, yb), :]
+        if c > 0:
+            overlap(c - 1)
+    overlap(chunks - 1)
+
+    count = bands * bands
+    flat = jnp.sum(part[...], axis=1)
+    if count < n:
+        flat = jnp.concatenate([flat, jnp.zeros((n - count, n), jnp.float32)], axis=0)
+    lanes = jnp.sum(flat.T, axis=0, keepdims=True)
+    sums_b[b] = jnp.broadcast_to(lanes, (8, n))
+
+    def sb_copy(target, owner):
+        return pltpu.make_async_remote_copy(
+            src_ref=sums_b.at[b], dst_ref=sums_b.at[owner],
+            send_sem=sb_send.at[target], recv_sem=sb_recv.at[owner],
+            device_id=(target, g), device_id_type=MESH,
+        )
+
+    def sg_copy(target, owner):
+        return pltpu.make_async_remote_copy(
+            src_ref=sums_g.at[g], dst_ref=sums_g.at[owner],
+            send_sem=sg_send.at[target], recv_sem=sg_recv.at[owner],
+            device_id=(b, target), device_id_type=MESH,
+        )
+
+    for d in range(1, bands):
+        sb_copy(lax.rem(b + d, bands), b).start()
+    for d in range(1, bands):
+        sb_copy(b, lax.rem(b + d, bands)).wait_recv()
+    sums_g[g] = jnp.sum(sums_b[...], axis=0)
+    for d in range(1, grids):
+        sg_copy(lax.rem(g + d, grids), g).start()
+    for d in range(1, grids):
+        sg_copy(g, lax.rem(g + d, grids)).wait_recv()
+    total = jnp.sum(sums_g[...], axis=0)[:1] * volume
+    splat[...] = jnp.broadcast_to(total, (n, n)).T
+
+    def entry(i, k):
+        first = splat[pl.ds(i * bands + k, 1), :]
+        return 0.5 * (first + splat[pl.ds(k * bands + i, 1), :])
+
+    factor = {}
+    inverse_diag = {}
+    for k in range(bands):
+        diag = entry(k, k)
+        for m in range(k):
+            diag = diag - factor[k, m] * factor[k, m]
+        inverse_diag[k] = 1.0 / jnp.sqrt(diag)
+        for i in range(k + 1, bands):
+            value = entry(i, k)
+            for m in range(k):
+                value = value - factor[i, m] * factor[k, m]
+            factor[i, k] = value * inverse_diag[k]
+    for k in range(bands):
+        splat[pl.ds(k * bands + k, 1), :] = inverse_diag[k]
+        for i in range(k + 1, bands):
+            splat[pl.ds(i * bands + k, 1), :] = factor[i, k]
+
+    def solve(x, _):
+        solved = []
+        for i in range(bands):
+            value = -tcol[i, x]
+            for k in range(i):
+                value = value - splat[pl.ds(i * bands + k, 1), :] * solved[k]
+            value = value * splat[pl.ds(i * bands + i, 1), :]
+            out[i, x] = value
+            solved.append(value)
+        return 0
+
+    lax.fori_loop(0, slab, solve, 0)
+
+    for c in range(chunks):
+        for d in range(nz):
+            @pl.when(jnp.logical_and(z - d >= 0, z + 1 < nz))
+            def _():
+                go_up(c, d).wait_send()
+
+            @pl.when(jnp.logical_and(z + d < nz, z > 0))
+            def _():
+                go_down(c, d).wait_send()
+
+            go_partner(c, d).wait_send()
+        for r in range(rounds):
+            for d in range(1, grids):
+                f_copy(c, r, lax.rem(g + d, grids), g).wait_send()
+                b_copy(c, r, lax.rem(g + d, grids), g).wait_send()
+        for d in range(1, bands):
+            t_copy(c, lax.rem(b + d, bands), b).wait_send()
+    for d in range(1, bands):
+        sb_copy(lax.rem(b + d, bands), b).wait_send()
+    for d in range(1, grids):
+        sg_copy(lax.rem(g + d, grids), g).wait_send()
+
+
+def fused(bands, grids, orbitals, sources):
+    n = orbitals.shape[2]
+    rounds = sources.shape[0]
+    slab = n // grids
+    depth = 8
+    chunks = slab // depth
+    yb = n // bands
+    numbers = np.arange(n)
+    angles = (numbers[:, None] * numbers[None, :] % n) * (2.0 * math.pi / n)
+    table = jnp.asarray(np.cos(angles) + np.sin(angles), jnp.float32)
+    high, low = parts_of(table)
+    left = jnp.block([[high, high], [low, low]])
+    right = jnp.block([[high, low], [high, low]])
+    signed = np.where(numbers < n // 2, numbers, numbers - n) * (2.0 * math.pi / n)
+    screen = (4.0 * math.pi / n) ** 2
+    waves = jnp.asarray(signed[:, None] ** 2 + signed[None, :] ** 2 + screen, jnp.float32)
+    volume = 1.0 / n**3
+    f32 = jnp.float32
+    dma = pltpu.SemaphoreType.DMA
+    scratch = [pltpu.VMEM((bands, depth, n, n), f32) for _ in range(chunks)]
+    scratch += [
+        pltpu.VMEM((chunks * rounds, n * depth, n), f32),
+        pltpu.VMEM((rounds, grids * chunks, (n // grids) * depth, n), f32),
+        pltpu.VMEM((chunks * rounds, n * depth, n), f32),
+        pltpu.VMEM((slab, n, n), f32),
+        pltpu.VMEM((bands, slab, yb, n), f32),
+        pltpu.VMEM((bands * bands, 8, n), f32),
+        pltpu.VMEM((bands, 8, n), f32),
+        pltpu.VMEM((grids, 8, n), f32),
+        pltpu.VMEM((n, n), f32),
+        dma((chunks,)),
+        dma((bands * chunks,)),
+        dma((bands * chunks,)),
+        dma((bands * chunks,)),
+        dma((bands * chunks,)),
+        dma((chunks * rounds * grids,)),
+        dma((chunks * rounds * grids,)),
+        dma((chunks * rounds * grids,)),
+        dma((chunks * rounds * grids,)),
+        dma((chunks * bands,)),
+        dma((chunks * bands,)),
+        dma((bands,)),
+        dma((bands,)),
+        dma((grids,)),
+        dma((grids,)),
+    ]
+    vmem = pl.BlockSpec(memory_space=pltpu.VMEM)
+    return pl.pallas_call(
+        functools.partial(whole_kernel, bands, grids, rounds, chunks, n, volume, screen),
+        out_shape=jax.ShapeDtypeStruct((bands, slab, yb, n), f32),
+        in_specs=[
+            pl.BlockSpec(memory_space=pltpu.SMEM),
+            pl.BlockSpec(memory_space=pl.ANY),
+            vmem, vmem, vmem,
+        ],
+        out_specs=vmem,
+        scratch_shapes=scratch,
+        compiler_params=pltpu.CompilerParams(
+            collective_id=0, has_side_effects=True, vmem_limit_bytes=60 * 1024 * 1024
+        ),
+        name="exchange",
+    )(sources, orbitals, left, right, waves)
+
+
+def per_device(orbitals, sources):
+    held, slab, full_y, full_z = orbitals.shape
+    bands = lax.axis_size("band")
+    grids = lax.axis_size("grid")
+    n = full_y
+    fits = (
+        held == 1 and n == full_z == slab * grids and n % 128 == 0 and slab % 8 == 0
+        and bands % 2 == 0 and bands * bands <= n and n % (8 * bands) == 0
+        and 4 * n * n * slab * (bands + 3 * sources.shape[0] + 3) <= 50 * 2**20
+    )
+    if fits:
+        return fused(bands, grids, orbitals, sources)
+    return general(orbitals, sources)
+
+
 def solution(mesh):
     placed = (P("band", "grid", None, None), P())
     return jax.shard_map(

time: 623 us -> 289 us (0.46); the launches traced: 616 us -> 289 us
  waiting for transfers between devices: 371 us -> 0 us
  Pallas kernels: 0 us -> 286 us
  matrix products: 84.1 us -> 0 us
  local copies, waits for them, and re-layouts: 52.8 us -> 3.05 us
  starting transfers between devices: 46.3 us -> 0 us
  blocking collectives: 36.8 us -> 0 us
  between operations: 16.8 us -> 0.01 us
  other arithmetic: 8.11 us -> 0 us
    pallas_call x0 -> x1, Pallas kernels: none -> 286 us  [fused(): pl.pallas_call(functools.partial(whole_kernel, bands, grids, rounds, chun...]
    all_to_all x10 -> x0, waiting for transfers between devices: 193 us -> none  [the longest x4 61.6 us: per_device(): lax.all_to_all(spectra, 'grid', split_axis=2, concat_axis=1, tiled=True)]
    psum x1 -> x0, waiting for transfers between devices: 178 us -> none  [spread_2(): return lax.psum(block, axis)]
    dot_general x25 -> x0, matrix products: 82.2 us -> none  [the longest x8 25.4 us: plane_transform(): return jnp.einsum('bxyk,yj->bxjk', spread, table_y, precision=highest)]
    all_to_all x10 -> x0, starting transfers between devices: 46.3 us -> none  [the longest x4 18.8 us: per_device(): lax.all_to_all(filtered, 'grid', split_axis=1, concat_axis=2, tiled=True)]
    psum x1 -> x0, blocking collectives: 36.8 us -> none  [per_device(): intersection = lax.psum(partial_intersection, ('band', 'grid'))]
    all_to_all x13 -> x0, local copies, waits for them, and re-layouts: 23.8 us -> none  [the longest x8 12.1 us: per_device(): lax.all_to_all(spectra, 'grid', split_axis=2, concat_axis=1, tiled=True)]
    transpose x8 -> x0, local copies, waits for them, and re-layouts: 20.5 us -> none  [the longest x4 10.2 us: plane_transform(): return jnp.einsum('bxyk,yj->bxjk', spread, table_y, precision=highest)]
  transfers between devices with their start and end apart: 11 -> 0, of which waited for: 11 -> 0; matrix products, arithmetic and copies ran while one was open for 16% -> 0% of each run, Pallas kernels for 0% -> 0%
where the time goes in v1:
time: 289 us
  Pallas kernels  286 us (99%)
  local copies, waits for them, and re-layouts  3.05 us (1%)
    pallas_call x1, Pallas kernels, fused(): pl.pallas_call(functools.partial(whole_kernel, bands, grids, rounds, chun...  286 us

profile of v1, /device:TPU:0, one launch (start us, length us, event | category | flops | bytes accessed | tf_op | source)
XLA Modules:
  0.0 288.9 jit_solution(12470450665592486591)
XLA Ops:
  0.0 285.8 %exchange.1 = f32[8,32,16,128]{3,2,1,0:T(8,128)} custom-call(s32[4]{0:T(128)} %sources.1, f32[1,32,128,128]{3,2,1,0:T(8,128)} %orbitals.1, bf16[256,256]{1,0:T(8,128)(2,1)} %constant.13.left_ref, bf16[256,256]{1,0:T(8,128)(2,1)} %constant.15.right_ref, f32[128,128]{1,0:T(8,128)} %constant.5.clone.waves_ref), custom_call_target="tpu_custom_call" | custom-call | tf_op jit(solution)/shard_map/exchange/pallas_call | solution.py:481
  285.8 3.0 %copy.6 = f32[8,32,16,128]{3,2,1,0:T(8,128)} copy(f32[8,32,16,128]{3,2,1,0:T(8,128)} %exchange.1) | data formatting | bytes 4194304

commit v2 on v1

--- a/solution.py
+++ b/solution.py
@@ -120,13 +120,13 @@
 
 
 def whole_kernel(
-    bands, grids, rounds, chunks, n, volume, screen,
+    bands, grids, rounds, chunks, unit, n, volume,
     sources, orbitals, left_ref, right_ref, waves_ref, out, *scratch,
 ):
-    gath = scratch[:chunks]
-    (spec, cols, back, terms, tcol, part, sums_b, sums_g, splat, in_sem,
-     g_recv, up_send, dn_send, pt_send, f_send, f_recv, b_send, b_recv,
-     t_send, t_recv, sb_send, sb_recv, sg_send, sg_recv) = scratch[chunks:]
+    (own, mate, up, dn, src, fcol, spec, cols, back, terms, tcol, part, sums_b, sums_g, splat,
+     in_sem, m_send, m_recv, up_send, up_recv, dn_send, dn_recv, s_send, s_recv,
+     o_send, o_recv, f_send, f_recv, b_send, b_recv,
+     t_send, t_recv, sb_send, sb_recv, sg_send, sg_recv) = scratch
     b = lax.axis_index("band")
     g = lax.axis_index("grid")
     nz = bands // 2
@@ -136,6 +136,9 @@
     ycols = n // grids
     piece = ycols * depth
     yb = n // bands
+    half = slab // 2
+    units = half // unit
+    total_units = rounds * units
     partner = z * 2 + (1 - core)
 
     barrier = pltpu.get_barrier_semaphore()
@@ -145,68 +148,97 @@
         pl.semaphore_signal(barrier, inc=1, device_id=(b, lax.rem(g + d, grids)), device_id_type=MESH)
     loads = [
         pltpu.make_async_copy(
-            orbitals.at[0, pl.ds(c * depth, depth)], gath[c].at[b], in_sem.at[c]
-        )
-        for c in range(chunks)
+            orbitals.at[0, pl.ds(h * half, half)], own.at[pl.ds(h * half, half)], in_sem.at[h]
+        )
+        for h in range(2)
     ]
     for load in loads:
         load.start()
+    for load in loads:
+        load.wait()
     pl.semaphore_wait(barrier, bands + grids - 2)
 
-    def slab_copy(c, origin, target, send):
-        return pltpu.make_async_remote_copy(
-            src_ref=gath[c].at[origin], dst_ref=gath[c].at[origin],
-            send_sem=send, recv_sem=g_recv.at[origin * chunks + c],
+    def mate_copy(u):
+        return pltpu.make_async_remote_copy(
+            src_ref=own.at[pl.ds((1 - core) * half + u * unit, unit)],
+            dst_ref=mate.at[pl.ds(u * unit, unit)],
+            send_sem=m_send.at[u], recv_sem=m_recv.at[u],
+            device_id=(partner, g), device_id_type=MESH,
+        )
+
+    def up_copy(v):
+        return pltpu.make_async_remote_copy(
+            src_ref=up.at[v], dst_ref=up.at[v],
+            send_sem=up_send.at[v], recv_sem=up_recv.at[v],
+            device_id=(lax.rem(b + 2, bands), g), device_id_type=MESH,
+        )
+
+    def dn_copy(v):
+        return pltpu.make_async_remote_copy(
+            src_ref=dn.at[v], dst_ref=dn.at[v],
+            send_sem=dn_send.at[v], recv_sem=dn_recv.at[v],
+            device_id=(lax.rem(b + bands - 2, bands), g), device_id_type=MESH,
+        )
+
+    def src_copy(v, side):
+        r, u = lax.div(v, units), lax.rem(v, units)
+        block = src.at[r, pl.ds(side * half + u * unit, unit)]
+        return pltpu.make_async_remote_copy(
+            src_ref=block, dst_ref=block,
+            send_sem=s_send.at[v], recv_sem=s_recv.at[v],
+            device_id=(partner, g), device_id_type=MESH,
+        )
+
+    for u in range(units):
+        mate_copy(u).start()
+
+    def step(t, _):
+        @pl.when(t < units)
+        def _():
+            mate_copy(t).wait_recv()
+
+        def pass_on(v, box, copy, first, last):
+            @pl.when(jnp.logical_and(v >= 0, v < total_units))
+            def _():
+                r, u = lax.div(v, units), lax.rem(v, units)
+                s = sources[r]
+                here = jnp.where(
+                    s == b, own[pl.ds(core * half + u * unit, unit)], mate[pl.ds(u * unit, unit)]
+                )
+
+                @pl.when(first)
+                def _():
+                    box[v] = here
+
+                @pl.when(jnp.logical_not(first))
+                def _():
+                    copy(v).wait_recv()
+                    box[v] = jnp.where(jnp.logical_or(s == b, s == partner), here, box[v])
+
+                @pl.when(jnp.logical_not(last))
+                def _():
+                    copy(v).start()
+
+        pass_on(t - z, up, up_copy, z == 0, z == nz - 1)
+        pass_on(t - (nz - 1 - z), dn, dn_copy, z == nz - 1, z == 0)
+        v = t - (nz - 1)
+
+        @pl.when(v >= 0)
+        def _():
+            r, u = lax.div(v, units), lax.rem(v, units)
+            src[r, pl.ds(core * half + u * unit, unit)] = jnp.where(
+                sources[r] < 2 * z + 2, up[v], dn[v]
+            )
+            src_copy(v, core).start()
+
+        return 0
+
+    def o_copy(target, owner):
+        return pltpu.make_async_remote_copy(
+            src_ref=own.at[:, pl.ds(target * yb, yb)], dst_ref=fcol.at[owner],
+            send_sem=o_send.at[target], recv_sem=o_recv.at[owner],
             device_id=(target, g), device_id_type=MESH,
         )
-
-    def go_up(c, d):
-        return slab_copy(c, (z - d) * 2 + core, (z + 1) * 2 + core, up_send.at[d * chunks + c])
-
-    def go_down(c, d):
-        return slab_copy(c, (z + d) * 2 + core, (z - 1) * 2 + core, dn_send.at[d * chunks + c])
-
-    def go_partner(c, zz):
-        return slab_copy(c, zz * 2 + core, partner, pt_send.at[zz * chunks + c])
-
-    def own_sends(c):
-        loads[c].wait()
-
-        @pl.when(z + 1 < nz)
-        def _():
-            go_up(c, 0).start()
-
-        @pl.when(z > 0)
-        def _():
-            go_down(c, 0).start()
-
-        go_partner(c, z).start()
-
-    def arrivals(c):
-        for d in range(1, nz):
-            @pl.when(z - d >= 0)
-            def _():
-                slab_copy(c, (z - d) * 2 + core, partner, pt_send.at[0]).wait_recv()
-
-                @pl.when(z + 1 < nz)
-                def _():
-                    go_up(c, d).start()
-
-                go_partner(c, z - d).start()
-
-            @pl.when(z + d < nz)
-            def _():
-                slab_copy(c, (z + d) * 2 + core, partner, pt_send.at[0]).wait_recv()
-
-                @pl.when(z > 0)
-                def _():
-                    go_down(c, d).start()
-
-                go_partner(c, z + d).start()
-
-    def partner_arrivals(c):
-        for zz in range(nz):
-            slab_copy(c, zz * 2 + (1 - core), partner, pt_send.at[0]).wait_recv()
 
     left = left_ref[...]
     right = right_ref[...]
@@ -229,40 +261,55 @@
             device_id=(b, target), device_id_type=MESH,
         )
 
-    own_sends(0)
-    for c in range(chunks):
-        arrivals(c)
-        if c + 1 < chunks:
-            own_sends(c + 1)
-        partner_arrivals(c)
-
-        def forward(r, _, c=c):
-            s = sources[r]
-            for k in range(0, depth, 2):
-                pair = gath[c][s, pl.ds(k, 2)] * gath[c][b, pl.ds(k, 2)]
-                rows = along_lanes(pair.reshape(2 * n, n), right)
-                planes = along_rows(left, rows[:n], rows[n:])
-                spec[c * rounds + r, pl.ds(k, n, stride=depth), :] = planes[:, :n]
-                spec[c * rounds + r, pl.ds(k + 1, n, stride=depth), :] = planes[:, n:]
-            for d in range(1, grids):
-                f_copy(c, r, lax.rem(g + d, grids), g).start()
-            cols[r, g * chunks + c] = spec[c * rounds + r, pl.ds(g * piece, piece), :]
+    base = waves_ref[...]
+    chunk_units = depth // unit
+
+    def forward_chunk(c, r):
+        for k in range(0, depth, 2):
+            at = c * depth + k
+            pair = src[r, pl.ds(at, 2)] * own[pl.ds(at, 2)]
+            rows = along_lanes(pair.reshape(2 * n, n), right)
+            planes = along_rows(left, rows[:n], rows[n:])
+            spec[c * rounds + r, pl.ds(k, n, stride=depth), :] = planes[:, :n]
+            spec[c * rounds + r, pl.ds(k + 1, n, stride=depth), :] = planes[:, n:]
+        for d in range(1, grids):
+            f_copy(c, r, lax.rem(g + d, grids), g).start()
+        cols[r, g * chunks + c] = spec[c * rounds + r, pl.ds(g * piece, piece), :]
+
+    def forward(r):
+        def phase(i, _):
+            start = r * units + i * chunk_units + (nz - 1)
+            if r == 0:
+                lax.fori_loop(jnp.where(i == 0, 0, start), start + chunk_units, step, 0)
+            else:
+                lax.fori_loop(start, start + chunk_units, step, 0)
+
+            def side(e, _):
+                @pl.when(e == 1)
+                def _():
+                    for u in range(chunk_units):
+                        src_copy(r * units + i * chunk_units + u, 1 - core).wait_recv()
+
+                where = jnp.where(e == 0, core, 1 - core)
+                forward_chunk(where * (chunks // 2) + i, r)
+                return 0
+
+            lax.fori_loop(0, 2, side, 0)
             return 0
 
-        lax.fori_loop(0, rounds, forward, 0)
-
-    base = waves_ref[...]
-    for r in range(rounds):
+        lax.fori_loop(0, chunks // 2, phase, 0)
+
+    def lines(r):
         for c in range(chunks):
             for d in range(1, grids):
                 f_copy(c, r, g, lax.rem(g + d, grids)).wait_recv()
 
-        def line(k, _, r=r):
-            lines = [
+        def line(k, _):
+            held = [
                 cols[r, :, pl.ds(pl.multiple_of((2 * k + e) * depth, depth), depth), :].reshape(n, n)
                 for e in range(2)
             ]
-            moved = along_rows(left, lines[0], lines[1])
+            moved = along_rows(left, held[0], held[1])
             filtered = []
             for e in range(2):
                 ky = g * ycols + 2 * k + e
@@ -277,12 +324,67 @@
             return 0
 
         lax.fori_loop(0, ycols // 2, line, 0)
+
+    def give_back(c, r):
         for d in range(1, grids):
-            b_copy(0, r, lax.rem(g + d, grids), g).start()
-    for c in range(1, chunks):
-        for r in range(rounds):
-            for d in range(1, grids):
-                b_copy(c, r, lax.rem(g + d, grids), g).start()
+            b_copy(c, r, lax.rem(g + d, grids), g).start()
+
+    def inverse(c, r):
+        for d in range(1, grids):
+            b_copy(c, r, g, lax.rem(g + d, grids)).wait_recv()
+        back[c * rounds + r, pl.ds(g * piece, piece), :] = cols[r, g * chunks + c]
+        for k in range(0, depth, 2):
+            planes = along_rows(
+                left,
+                back[c * rounds + r, pl.ds(k, n, stride=depth), :],
+                back[c * rounds + r, pl.ds(k + 1, n, stride=depth), :],
+            )
+            rows = jnp.concatenate([planes[:, :n], planes[:, n:]], axis=0)
+            potential = along_lanes(rows, right).reshape(2, n, n)
+            at = c * depth + k
+            here = src[r, pl.ds(at, 2)] * potential
+            if r == 0:
+                terms[pl.ds(at, 2)] = here
+            else:
+                terms[pl.ds(at, 2)] += here
+
+    def inverse_all(r):
+        def one(c, _):
+            inverse(c, r)
+            return 0
+
+        lax.fori_loop(0, chunks, one, 0)
+
+    tail = min(2, rounds)
+    returned = 0
+    for r in range(rounds):
+        forward(r)
+        if r == rounds - 1:
+            for d in range(1, bands):
+                o_copy(lax.rem(b + d, bands), b).start()
+        if r % 2 == 1 and returned < rounds - tail:
+            lines(returned)
+            for c in range(chunks):
+                give_back(c, returned)
+            returned += 1
+            ready = returned - 1
+            if ready > 0:
+                inverse_all(ready - 1)
+    while returned < rounds - tail:
+        lines(returned)
+        for c in range(chunks):
+            give_back(c, returned)
+        returned += 1
+        if returned > 1:
+            inverse_all(returned - 2)
+    for r in range(rounds - tail, rounds):
+        lines(r)
+    for c in range(chunks):
+        for r in range(rounds - tail, rounds):
+            give_back(c, r)
+    fcol[b] = own[:, pl.ds(b * yb, yb), :]
+    if rounds > tail:
+        inverse_all(rounds - tail - 1)
 
     def t_copy(c, target, owner):
         return pltpu.make_async_remote_copy(
@@ -298,7 +400,7 @@
             t_copy(c, b, lax.rem(b + d, bands)).wait_recv()
 
         def one(i, _):
-            mine = gath[c][i, :, pl.ds(b * yb, yb), :]
+            mine = fcol[i, pl.ds(c * depth, depth)]
             for k in range(bands):
                 prod = mine * tcol[k, pl.ds(c * depth, depth)]
                 total = jnp.sum(prod.reshape(-1, 8, n), axis=0)
@@ -311,32 +413,14 @@
         lax.fori_loop(0, bands, one, 0)
 
     for c in range(chunks):
-        for r in range(rounds):
-            for d in range(1, grids):
-                b_copy(c, r, g, lax.rem(g + d, grids)).wait_recv()
-            back[c * rounds + r, pl.ds(g * piece, piece), :] = cols[r, g * chunks + c]
-            s = sources[r]
-
-            def inverse(k, _, c=c, r=r, s=s):
-                planes = along_rows(
-                    left,
-                    back[c * rounds + r, pl.ds(2 * k, n, stride=depth), :],
-                    back[c * rounds + r, pl.ds(2 * k + 1, n, stride=depth), :],
-                )
-                rows = jnp.concatenate([planes[:, :n], planes[:, n:]], axis=0)
-                potential = along_lanes(rows, right).reshape(2, n, n)
-                here = gath[c][s, pl.ds(2 * k, 2)] * potential
-                if r == 0:
-                    terms[pl.ds(c * depth + 2 * k, 2)] = here
-                else:
-                    terms[pl.ds(c * depth + 2 * k, 2)] += here
-                return 0
-
-            for k in range(depth // 2):
-                inverse(k, 0)
+        for r in range(rounds - tail, rounds):
+            inverse(c, r)
         for d in range(1, bands):
             t_copy(c, lax.rem(b + d, bands), b).start()
         tcol[b, pl.ds(c * depth, depth)] = terms[pl.ds(c * depth, depth), pl.ds(b * yb, yb), :]
+        if c == 1:
+            for d in range(1, bands):
+                o_copy(b, lax.rem(b + d, bands)).wait_recv()
         if c > 0:
             overlap(c - 1)
     overlap(chunks - 1)
@@ -408,17 +492,25 @@
 
     lax.fori_loop(0, slab, solve, 0)
 
+    for u in range(units):
+        mate_copy(u).wait_send()
+
+    def settle(v, _):
+        @pl.when(z < nz - 1)
+        def _():
+            up_copy(v).wait_send()
+
+        @pl.when(z > 0)
+        def _():
+            dn_copy(v).wait_send()
+
+        src_copy(v, core).wait_send()
+        return 0
+
+    lax.fori_loop(0, total_units, settle, 0)
+    for d in range(1, bands):
+        o_copy(lax.rem(b + d, bands), b).wait_send()
     for c in range(chunks):
-        for d in range(nz):
-            @pl.when(jnp.logical_and(z - d >= 0, z + 1 < nz))
-            def _():
-                go_up(c, d).wait_send()
-
-            @pl.when(jnp.logical_and(z + d < nz, z > 0))
-            def _():
-                go_down(c, d).wait_send()
-
-            go_partner(c, d).wait_send()
         for r in range(rounds):
             for d in range(1, grids):
                 f_copy(c, r, lax.rem(g + d, grids), g).wait_send()
@@ -450,8 +542,16 @@
     volume = 1.0 / n**3
     f32 = jnp.float32
     dma = pltpu.SemaphoreType.DMA
-    scratch = [pltpu.VMEM((bands, depth, n, n), f32) for _ in range(chunks)]
-    scratch += [
+    unit = 2
+    units = slab // 2 // unit
+    relay = rounds * units
+    scratch = [
+        pltpu.VMEM((slab, n, n), f32),
+        pltpu.VMEM((slab // 2, n, n), f32),
+        pltpu.VMEM((relay, unit, n, n), f32),
+        pltpu.VMEM((relay, unit, n, n), f32),
+        pltpu.VMEM((rounds, slab, n, n), f32),
+        pltpu.VMEM((bands, slab, yb, n), f32),
         pltpu.VMEM((chunks * rounds, n * depth, n), f32),
         pltpu.VMEM((rounds, grids * chunks, (n // grids) * depth, n), f32),
         pltpu.VMEM((chunks * rounds, n * depth, n), f32),
@@ -461,11 +561,17 @@
         pltpu.VMEM((bands, 8, n), f32),
         pltpu.VMEM((grids, 8, n), f32),
         pltpu.VMEM((n, n), f32),
-        dma((chunks,)),
-        dma((bands * chunks,)),
-        dma((bands * chunks,)),
-        dma((bands * chunks,)),
-        dma((bands * chunks,)),
+        dma((2,)),
+        dma((units,)),
+        dma((units,)),
+        dma((relay,)),
+        dma((relay,)),
+        dma((relay,)),
+        dma((relay,)),
+        dma((relay,)),
+        dma((relay,)),
+        dma((bands,)),
+        dma((bands,)),
         dma((chunks * rounds * grids,)),
         dma((chunks * rounds * grids,)),
         dma((chunks * rounds * grids,)),
@@ -479,7 +585,7 @@
     ]
     vmem = pl.BlockSpec(memory_space=pltpu.VMEM)
     return pl.pallas_call(
-        functools.partial(whole_kernel, bands, grids, rounds, chunks, n, volume, screen),
+        functools.partial(whole_kernel, bands, grids, rounds, chunks, unit, n, volume),
         out_shape=jax.ShapeDtypeStruct((bands, slab, yb, n), f32),
         in_specs=[
             pl.BlockSpec(memory_space=pltpu.SMEM),
@@ -501,9 +607,9 @@
     grids = lax.axis_size("grid")
     n = full_y
     fits = (
-        held == 1 and n == full_z == slab * grids and n % 128 == 0 and slab % 8 == 0
+        held == 1 and n == full_z == slab * grids and n % 128 == 0 and slab % 16 == 0
         and bands % 2 == 0 and bands * bands <= n and n % (8 * bands) == 0
-        and 4 * n * n * slab * (bands + 3 * sources.shape[0] + 3) <= 50 * 2**20
+        and 4 * n * n * slab * (5 * sources.shape[0] + 6) <= 54 * 2**20
     )
     if fits:
         return fused(bands, grids, orbitals, sources)

time: 289 us -> 265 us (0.917)
  Pallas kernels: 286 us -> 262 us
    pallas_call x1, Pallas kernels: 286 us -> 262 us  [fused(): pl.pallas_call(functools.partial(whole_kernel, bands, grids, rounds, chun...]
where the time goes in v2:
time: 265 us
  Pallas kernels  262 us (99%)
  local copies, waits for them, and re-layouts  3.05 us (1%)
    pallas_call x1, Pallas kernels, fused(): pl.pallas_call(functools.partial(whole_kernel, bands, grids, rounds, chun...  262 us

profile of v2, /device:TPU:0, one launch (start us, length us, event | category | flops | bytes accessed | tf_op | source)
XLA Modules:
  0.0 264.9 jit_solution(17020721576572841318)
XLA Ops:
  0.0 261.9 %exchange.1 = f32[8,32,16,128]{3,2,1,0:T(8,128)} custom-call(s32[4]{0:T(128)} %sources.1, f32[1,32,128,128]{3,2,1,0:T(8,128)} %orbitals.1, bf16[256,256]{1,0:T(8,128)(2,1)} %constant.13.left_ref, bf16[256,256]{1,0:T(8,128)(2,1)} %constant.15.right_ref, f32[128,128]{1,0:T(8,128)} %constant.5.clone.waves_ref), custom_call_target="tpu_custom_call" | custom-call | tf_op jit(solution)/shard_map/exchange/pallas_call | solution.py:587
  261.9 3.0 %copy.6 = f32[8,32,16,128]{3,2,1,0:T(8,128)} copy(f32[8,32,16,128]{3,2,1,0:T(8,128)} %exchange.1) | data formatting | bytes 4194304

commit v3 on v2

--- a/solution.py
+++ b/solution.py
@@ -120,7 +120,7 @@
 
 
 def whole_kernel(
-    bands, grids, rounds, chunks, unit, n, volume,
+    bands, grids, rounds, chunks, unit, ahead, n, volume,
     sources, orbitals, left_ref, right_ref, waves_ref, out, *scratch,
 ):
     (own, mate, up, dn, src, fcol, spec, cols, back, terms, tcol, part, sums_b, sums_g, splat,
@@ -139,6 +139,7 @@
     half = slab // 2
     units = half // unit
     total_units = rounds * units
+    lag = (nz - 1) * ahead
     partner = z * 2 + (1 - core)
 
     barrier = pltpu.get_barrier_semaphore()
@@ -219,9 +220,9 @@
                 def _():
                     copy(v).start()
 
-        pass_on(t - z, up, up_copy, z == 0, z == nz - 1)
-        pass_on(t - (nz - 1 - z), dn, dn_copy, z == nz - 1, z == 0)
-        v = t - (nz - 1)
+        pass_on(t - z * ahead, up, up_copy, z == 0, z == nz - 1)
+        pass_on(t - (nz - 1 - z) * ahead, dn, dn_copy, z == nz - 1, z == 0)
+        v = t - lag
 
         @pl.when(v >= 0)
         def _():
@@ -278,7 +279,7 @@
 
     def forward(r):
         def phase(i, _):
-            start = r * units + i * chunk_units + (nz - 1)
+            start = r * units + i * chunk_units + lag
             if r == 0:
                 lax.fori_loop(jnp.where(i == 0, 0, start), start + chunk_units, step, 0)
             else:
@@ -585,7 +586,7 @@
     ]
     vmem = pl.BlockSpec(memory_space=pltpu.VMEM)
     return pl.pallas_call(
-        functools.partial(whole_kernel, bands, grids, rounds, chunks, unit, n, volume),
+        functools.partial(whole_kernel, bands, grids, rounds, chunks, unit, 2, n, volume),
         out_shape=jax.ShapeDtypeStruct((bands, slab, yb, n), f32),
         in_specs=[
             pl.BlockSpec(memory_space=pltpu.SMEM),

time: 265 us -> 246 us (0.928)
  Pallas kernels: 262 us -> 243 us
    pallas_call x1, Pallas kernels: 262 us -> 243 us  [fused(): pl.pallas_call(functools.partial(whole_kernel, bands, grids, rounds, chun...]
where the time goes in v3:
time: 246 us
  Pallas kernels  243 us (99%)
  local copies, waits for them, and re-layouts  3.05 us (1%)
    pallas_call x1, Pallas kernels, fused(): pl.pallas_call(functools.partial(whole_kernel, bands, grids, rounds, chun...  243 us

profile of v3, /device:TPU:0, one launch (start us, length us, event | category | flops | bytes accessed | tf_op | source)
XLA Modules:
  0.0 246.0 jit_solution(13523174290146528296)
XLA Ops:
  0.0 243.0 %exchange.1 = f32[8,32,16,128]{3,2,1,0:T(8,128)} custom-call(s32[4]{0:T(128)} %sources.1, f32[1,32,128,128]{3,2,1,0:T(8,128)} %orbitals.1, bf16[256,256]{1,0:T(8,128)(2,1)} %constant.13.left_ref, bf16[256,256]{1,0:T(8,128)(2,1)} %constant.15.right_ref, f32[128,128]{1,0:T(8,128)} %constant.5.clone.waves_ref), custom_call_target="tpu_custom_call" | custom-call | tf_op jit(solution)/shard_map/exchange/pallas_call | solution.py:588
  243.0 3.0 %copy.6 = f32[8,32,16,128]{3,2,1,0:T(8,128)} copy(f32[8,32,16,128]{3,2,1,0:T(8,128)} %exchange.1) | data formatting | bytes 4194304
